TPU v7x, 32 devices: a whole 2x2x4 slice. The times are simulated.
32 devices in a mesh: blade: 4 (over y, x), dp: 8 (over z, core).
Axes of the slice: x: 2, y: 2, z: 4, core: 2. Of those that a mesh axis runs over, the one named last changes fastest.
Arguments:
- inputs: bfloat16 [64, 4, 48, 4096], P('dp', 'blade'), may hold values from -6 to 6
- cotangent: bfloat16 [64, 4, 48, 4096], P('dp', 'blade'), may hold values from -6 to 6
- norm_table: float32 [16], replicated, may hold values from 0.5 to 2
- sample_index: int32 [64], P('dp'), may hold values from 0 to 15
- spec_weight: float32 [4, 256, 2, 48, 48], P('blade', 'dp'), may hold values from -0.875 to 0.875
- spec_first: float32 [4, 256, 2, 48, 48], P('blade', 'dp'), may hold values from -6 to 6
- spec_second: float32 [4, 256, 2, 48, 48], P('blade', 'dp'), may hold values from 0.32 to 1.344
- lin_weight: float32 [4, 48, 48], P('blade'), may hold values from -0.4375 to 0.4375
- lin_first: float32 [4, 48, 48], P('blade'), may hold values from -640 to 640
- lin_second: float32 [4, 48, 48], P('blade'), may hold values from 786.432 to 3145.728
Outputs:
- output: bfloat16 [64, 4, 48, 4096], P('dp', 'blade')
- input_grad: float32 [64, 4, 48, 4096], P('dp', 'blade')
- spec_new: float32 [4, 256, 2, 48, 48], P('blade', 'dp')
- spec_first_new: float32 [4, 256, 2, 48, 48], P('blade', 'dp')
- spec_second_new: float32 [4, 256, 2, 48, 48], P('blade', 'dp')
- lin_new: float32 [4, 48, 48], P('blade')
- lin_first_new: float32 [4, 48, 48], P('blade')
- lin_second_new: float32 [4, 48, 48], P('blade')
All inputs are finite; a program needn't handle non-finite values.
Results may differ from a plain program's by a relative error of at most 0.014.
Values may be sent and summed in bfloat16 or wider, within the bound.
No kernel may reach another device: no remote copies, remote signals or barrier semaphores. Data moves between devices by JAX's collectives and lax.ppermute only.
A program may use at most 192 MiB of HBM per device.

v0:
```python
from functools import partial
import math
import jax
import jax.numpy as jnp
from jax import lax
from jax.sharding import PartitionSpec as P

GRID = 64
MSIDE = 16
NTAB = 16
STEP_COUNT = 5
NPIX = 4096
MODES = 256
BETA_ONE = 0.9
BETA_TWO = 0.999
EPSILON = 1e-08
RATE = 0.1
DECAY = 0.01


def blade_sign(left_blade, right_blade):
    return 1 - 2 * (left_blade // 2 % 2) * (right_blade % 2)


def tables():
    pix_ids = jnp.arange(NPIX, dtype=jnp.int32)
    pix_row = pix_ids // GRID
    pix_col = pix_ids % GRID
    mode_ids = jnp.arange(MODES, dtype=jnp.int32)
    row_index = mode_ids // MSIDE
    col_freq = mode_ids % MSIDE
    row_freq = jnp.where(row_index < MSIDE // 2, row_index, GRID - MSIDE + row_index)
    phase_int = (pix_row[:, None] * row_freq[None, :] + pix_col[:, None] * col_freq[None, :]) % GRID
    angles = phase_int.astype(jnp.float32) * (2.0 * math.pi / GRID)
    forward = jnp.concatenate([jnp.cos(angles), -jnp.sin(angles)], axis=1) / GRID
    factor = jnp.where(col_freq == 0, 1.0, 2.0).astype(jnp.float32)
    factor = jnp.concatenate([factor, factor])
    return (forward.astype(jnp.bfloat16), (forward * factor[None, :]).astype(jnp.bfloat16))


def sign_matrix(own_blade, first_side):
    lane_ids = jnp.arange(4, dtype=jnp.int32)
    row_ids = lane_ids[:, None]
    col_ids = lane_ids[None, :]
    matches = jnp.bitwise_xor(row_ids, col_ids) == own_blade
    if first_side == "col":
        values = blade_sign(col_ids, own_blade)
    elif first_side == "row":
        values = blade_sign(row_ids, col_ids)
    else:
        values = blade_sign(own_blade, col_ids)
    return jnp.where(matches, values, 0).astype(jnp.bfloat16)


def adamw(weight, first, second, grad):
    first_new = BETA_ONE * first + (1.0 - BETA_ONE) * grad
    second_new = BETA_TWO * second + (1.0 - BETA_TWO) * grad * grad
    corr_one = 1.0 - BETA_ONE**STEP_COUNT
    corr_two = 1.0 - BETA_TWO**STEP_COUNT
    update = first_new / corr_one / (jnp.sqrt(second_new / corr_two) + EPSILON)
    return (weight - RATE * (update + DECAY * weight), first_new, second_new)


def body(
    inputs,
    cotangent,
    norm_table,
    sample_index,
    spec_weight,
    spec_first,
    spec_second,
    lin_weight,
    lin_first,
    lin_second,
):
    own_blade = lax.axis_index("blade")
    num_samples = inputs.shape[0]
    num_chans = inputs.shape[2]
    forward_table, inverse_table = tables()
    matches = sample_index[:, None] == jnp.arange(NTAB, dtype=jnp.int32)[None, :]
    normalizer = jnp.sum(jnp.where(matches, norm_table[None, :], 0.0), axis=1)[:, None, None, None]
    normed = inputs.astype(jnp.float32) / normalizer
    normed_low = normed.astype(jnp.bfloat16)
    lin_low = lin_weight.astype(jnp.bfloat16)
    spec_low = spec_weight.astype(jnp.bfloat16)
    own_modes = jnp.einsum(
        "sjcp,pn->sjcn", normed_low, forward_table, preferred_element_type=jnp.float32
    ).astype(jnp.bfloat16)
    normed_all, lin_all, modes_all = (
        lax.all_gather(normed_low, "blade", axis=1, tiled=True),
        lax.all_gather(lin_low, "blade", axis=0, tiled=True),
        lax.all_gather(own_modes, "blade", axis=1, tiled=True),
    )
    modes_real = modes_all[..., :MODES]
    modes_imag = modes_all[..., MODES:]
    block_in = lax.all_gather(spec_low, "dp", axis=1, tiled=True)
    w_real = block_in[0, :, 0]
    w_imag = block_in[0, :, 1]
    form = partial(jnp.einsum, "sjcm,mco->sjom", preferred_element_type=jnp.float32)
    out_real = form(modes_real, w_real) - form(modes_imag, w_imag)
    out_imag = form(modes_real, w_imag) + form(modes_imag, w_real)
    products = jnp.stack([out_real, out_imag], axis=3)
    blade_mix = sign_matrix(own_blade, "col")
    partial_spec = jnp.einsum("ij,sjcrm->sicrm", blade_mix.astype(jnp.float32), products)
    spec_sum = lax.psum_scatter(partial_spec, "blade", scatter_dimension=1, tiled=True)
    spec_out = spec_sum.reshape(num_samples, 1, num_chans, 2 * MODES).astype(jnp.bfloat16)
    spatial = jnp.einsum(
        "sjcn,pn->sjcp", spec_out, inverse_table, preferred_element_type=jnp.float32
    )
    forward_lin = sign_matrix(own_blade, "row")
    lin_cat = jnp.einsum(
        "jk,kco->jco", forward_lin, lin_all, preferred_element_type=jnp.float32
    ).astype(jnp.bfloat16)
    linear = jnp.einsum("sjcp,jco->sop", normed_all, lin_cat, preferred_element_type=jnp.float32)[
        :, None
    ]
    pre = spatial + linear
    activated, gelu_pullback = jax.vjp(partial(jax.nn.gelu, approximate=False), pre)
    output = (normed + activated).astype(jnp.bfloat16)
    cot_float = cotangent.astype(jnp.float32)
    grad_pre = gelu_pullback(cot_float)[0].astype(jnp.bfloat16)
    grad_spec = jnp.einsum(
        "sjcp,pn->sjcn", grad_pre, inverse_table, preferred_element_type=jnp.float32
    ).astype(jnp.bfloat16)
    pre_all, spec_grad_all = (
        lax.all_gather(grad_pre, "blade", axis=1, tiled=True),
        lax.all_gather(grad_spec, "blade", axis=1, tiled=True),
    )
    mixed_spec = jnp.einsum(
        "ij,sicn->sjcn", blade_mix, spec_grad_all, preferred_element_type=jnp.float32
    ).astype(jnp.bfloat16)
    mixed_pre = jnp.einsum(
        "ij,sicp->sjcp", blade_mix, pre_all, preferred_element_type=jnp.float32
    ).astype(jnp.bfloat16)
    grad_real = mixed_spec[..., :MODES]
    grad_imag = mixed_spec[..., MODES:]
    d_real = grad_real
    d_imag = grad_imag
    form = partial(jnp.einsum, "sjcm,sjom->mco", preferred_element_type=jnp.float32)
    term_real = form(modes_real, d_real) + form(modes_imag, d_imag)
    term_imag = form(modes_real, d_imag) - form(modes_imag, d_real)
    spec_grad = lax.psum_scatter(
        jnp.stack([term_real, term_imag], axis=1).astype(jnp.bfloat16),
        "dp",
        scatter_dimension=0,
        tiled=True,
    ).astype(jnp.float32)[None]
    block_in = lax.all_gather(spec_low, "dp", axis=1, tiled=True)
    d_real = grad_real
    d_imag = grad_imag
    w_real = block_in[0, :, 0]
    w_imag = block_in[0, :, 1]
    form = partial(jnp.einsum, "sjom,mco->sjcm", preferred_element_type=jnp.float32)
    back_real = form(d_real, w_real) + form(d_imag, w_imag)
    back_imag = form(d_imag, w_real) - form(d_real, w_imag)
    back_all = jnp.stack([back_real, back_imag], axis=3)
    grad_modes = lax.psum_scatter(
        back_all.astype(jnp.bfloat16), "blade", scatter_dimension=1, tiled=True
    ).astype(jnp.float32)
    grad_modes = grad_modes.reshape(num_samples, 1, num_chans, 2 * MODES).astype(jnp.bfloat16)
    from_spec = jnp.einsum(
        "sjcn,pn->sjcp", grad_modes, forward_table, preferred_element_type=jnp.float32
    )
    lin_grad = jnp.einsum(
        "sjcp,sjop->co", normed_all, mixed_pre, preferred_element_type=jnp.float32
    )[None]
    lin_grad = lax.psum(lin_grad, "dp")
    back_lin = sign_matrix(own_blade, "own")
    lin_sel = jnp.einsum(
        "ik,kco->ico", back_lin, lin_all, preferred_element_type=jnp.float32
    ).astype(jnp.bfloat16)
    from_lin = jnp.einsum("siop,ico->scp", pre_all, lin_sel, preferred_element_type=jnp.float32)[
        :, None
    ]
    input_grad = (cot_float + from_lin + from_spec) / normalizer
    spec_new, spec_first_new, spec_second_new = adamw(
        spec_weight, spec_first, spec_second, spec_grad
    )
    lin_new, lin_first_new, lin_second_new = adamw(lin_weight, lin_first, lin_second, lin_grad)
    return (
        output,
        input_grad,
        spec_new,
        spec_first_new,
        spec_second_new,
        lin_new,
        lin_first_new,
        lin_second_new,
    )


def solution(mesh):
    return jax.shard_map(
        body,
        mesh=mesh,
        in_specs=(
            P("dp", "blade", None, None),
            P("dp", "blade", None, None),
            P(),
            P("dp"),
            P("blade", "dp", None, None, None),
            P("blade", "dp", None, None, None),
            P("blade", "dp", None, None, None),
            P("blade", None, None),
            P("blade", None, None),
            P("blade", None, None),
        ),
        out_specs=(
            P("dp", "blade", None, None),
            P("dp", "blade", None, None),
            P("blade", "dp", None, None, None),
            P("blade", "dp", None, None, None),
            P("blade", "dp", None, None, None),
            P("blade", None, None),
            P("blade", None, None),
            P("blade", None, None),
        ),
        check_vma=False,
    )
```

profile of v0, /device:TPU:0, one launch (start us, length us, event | category | flops | bytes accessed | tf_op | source)
XLA Modules:
  0.0 696.8 jit_solution(13028528623821768969)
XLA Ops:
  8.1 2.7 fusion.30
  10.8 16.9 %fusion.38 = (f32[4096,256]{1,0:T(8,128)S(1)}, f32[4096,256]{1,0:T(8,128)S(1)}) fusion(s32[256]{0:T(256)S(1)} %get-tuple-element.66, s32[4096]{0:T(1024)S(1)} %get-tuple-element.63, s32[256]{0:T(256)S(1)} %get-tuple-element.65, s32[4096]{0:T(1024)S(1)} %get-tuple-element.64), kind=kLoop, calls=%fused_computation.71 | loop fusion | flops 17825792 | bytes 8423424 | tf_op jit(solution)/shard_map/cos | solution.py:35
  27.8 2.0 copy-done.9
  31.0 2.6 fusion.53
  33.7 2.4 copy.254
  36.3 31.1 %all-gather.14.cloned.1.call-done = bf16[8,192,512]{2,1,0:T(8,128)(2,1)} async-done(((bf16[8,48,512]{2,1,0:T(8,128)(2,1)}), bf16[8,192,512]{2,1,0:T(8,128)(2,1)}) %all-gather.14.cloned.1.call-update) | async-done | bytes 1572880 | tf_op jit(solution)/shard_map/all_gather | solution.py:92
  67.4 2.4 fusion.118
  69.8 3.9 copy.222
  73.7 3.8 copy.223
  77.5 56.9 %all-gather.8.cloned.1.call-done = bf16[1,256,2,48,48]{4,3,1,2,0:T(8,128)(2,1)} async-done(((bf16[1,32,2,48,48]{4,3,1,2,0:T(8,128)(2,1)}), bf16[1,256,2,48,48]{4,3,1,2,0:T(8,128)(2,1)}) %all-gather.8.cloned.1.call-update) | async-done | bytes 2359312 | tf_op jit(solution)/shard_map/all_gather | solution.py:96
  134.4 3.0 fusion.42
  141.6 3.0 pad_maximum_fusion.1
  144.5 6.7 copy.169
  152.3 2.6 copy.171
  155.7 8.6 %all_gather.21 = bf16[4,48,48]{2,1,0:T(8,128)(2,1)S(1)} all-gather(bf16[1,48,48]{2,1,0:T(8,128)(2,1)S(1)} %convert_element_type.106), channel_id=1, replica_groups=mesh['blade'=4,'dp'=8] {'blade'}, dimensions={0}, use_global_device_ids=true | all-gather | bytes 23040 | tf_op jit(solution)/shard_map/all_gather | solution.py:91
  164.7 33.1 %reduce-scatter.12.cloned.1.call-done = f32[8,1,48,2,256]{4,2,3,0,1:T(8,128)} async-done(((f32[8,4,48,2,256]{4,2,3,0,1:T(8,128)}), f32[8,1,48,2,256]{4,2,3,0,1:T(8,128)}) %reduce-scatter.12.cloned.1.call-update) | async-done | bytes 786448
  199.5 8.9 %fusion.66 = f32[8,48,4096]{2,1,0:T(8,128)} fusion(bf16[8,48,512]{2,1,0:T(8,128)(2,1)S(1)} %convert_element_type.103, f32[4096,256]{1,0:T(8,128)} %copy-done.10, f32[4096,256]{1,0:T(8,128)} %copy-done.9, f32[512]{0:T(512)S(1)} %maximum_multiply_fusion), kind=kOutput, calls=%fused_computation.97 | convolution fusion | flops 1616904192 | bytes 15075328 | tf_op jit(solution)/shard_map/sjcn,pn->sjcp/dot_general | solution.py:107
  208.4 113.6 %all-gather.10.cloned.1.call-done = bf16[8,4,48,4096]{3,2,0,1:T(8,128)(2,1)} async-done(((bf16[8,1,48,4096]{3,2,0,1:T(8,128)(2,1)}), bf16[8,4,48,4096]{3,2,0,1:T(8,128)(2,1)}) %all-gather.10.cloned.1.call-update) | async-done | bytes 12582928 | tf_op jit(solution)/shard_map/all_gather | solution.py:90
  322.0 21.2 %fusion.12 = (bf16[8,1,48,4096]{3,2,0,1:T(8,128)(2,1)S(1)}, f32[8,48,4096]{2,1,0:T(8,128)}, f32[8,48,4096]{2,1,0:T(8,128)}) fusion(bf16[8,1,48,4096]{3,2,1,0:T(8,128)(2,1)} %param.11, f32[8,48,4096]{2,1,0:T(8,128)} %fusion.66, bf16[8,4,48,4096]{3,2,0,1:T(8,128)(2,1)} %all-gather.10.cloned.1.call-done, bf16[4,48,48]{1,2,0:T(8,128)(2,1)S(1)} %copy.175), kind=kOutput, calls=%fused_computation.19 | convolution fusion | flops 720371712 | bytes 37767168 | tf_op jit(solution)/shard_map/sjcp,jco->sop/dot_general | solution.py:114
  343.2 7.1 %fusion.56 = bf16[8,48,512]{2,1,0:T(8,128)(2,1)} fusion(bf16[8,1,48,4096]{3,2,0,1:T(8,128)(2,1)S(1)} %get-tuple-element.54, f32[4096,256]{1,0:T(8,128)} %copy-done.10, f32[4096,256]{1,0:T(8,128)} %copy-done.9, f32[512]{0:T(512)S(1)} %maximum_multiply_fusion), kind=kOutput, calls=%fused_computation.92 | convolution fusion | flops 1617100800 | bytes 11929600 | tf_op jit(solution)/shard_map/sjcp,pn->sjcn/dot_general | solution.py:122
  350.8 30.7 %all-gather.16.cloned.1.call-done = bf16[8,192,512]{2,1,0:T(8,128)(2,1)} async-done(((bf16[8,48,512]{2,1,0:T(8,128)(2,1)}), bf16[8,192,512]{2,1,0:T(8,128)(2,1)}) %all-gather.16.cloned.1.call-update) | async-done | bytes 1572880 | tf_op jit(solution)/shard_map/all_gather | solution.py:127
  381.5 2.8 fusion.50
  384.2 1.6 fusion.117
  385.9 5.4 copy.184
  391.2 4.0 copy.183
  395.2 4.4 fusion.39
  399.7 1.7 fusion.40
  401.4 1.8 fusion.44
  403.2 1.8 fusion.43
  405.0 2.9 pad_maximum_fusion.3
  407.8 5.5 copy.187
  413.6 2.8 fusion.120
  420.8 1.4 pad_maximum_fusion.2
  422.2 3.7 copy.220
  425.9 12.8 %reshape.319 = bf16[256,4608]{1,0:T(8,128)(2,1)} reshape(bf16[256,2,48,48]{3,2,1,0:T(8,128)(2,1)} %copy.220) | data formatting | bytes 4718592
  440.6 8.3 %fusion.37 = bf16[8,1,48,4096]{3,2,1,0:T(8,128)(2,1)} fusion(f32[8,48,4096]{2,1,0:T(8,128)} %get-tuple-element.55, f32[8,48,4096]{2,1,0:T(8,128)} %get-tuple-element.62, f32[8]{0:T(128)S(1)} %select_reduce_fusion, bf16[8,1,48,4096]{3,2,1,0:T(8,128)(2,1)S(1)} %copy-done.12), kind=kLoop, calls=%fused_computation.69 | loop fusion | flops 9437184 | bytes 18874400
  450.4 8.3 %fusion.62 = f32[8,48,4096]{2,1,0:T(8,128)} fusion(bf16[8,48,512]{2,1,0:T(8,128)(2,1)S(1)} %convert_element_type.117, f32[4096,256]{1,0:T(8,128)} %copy-done.10, f32[4096,256]{1,0:T(8,128)} %copy-done.9), kind=kOutput, calls=%fused_computation.96 | convolution fusion | flops 1616904192 | bytes 15073280 | tf_op jit(solution)/shard_map/sjcn,pn->sjcp/dot_general | solution.py:161
  458.7 24.2 %reduce-scatter.10.cloned.1.call-done = bf16[32,4608]{1,0:T(8,128)(2,1)} async-done(((bf16[256,4608]{1,0:T(8,128)(2,1)}), bf16[32,4608]{1,0:T(8,128)(2,1)}) %reduce-scatter.10.cloned.1.call-update) | async-done | bytes 294928
  483.0 1.7 reshape.320
  484.7 3.1 multiply_subtract_fusion
  487.8 1.3 copy.201
  489.1 1.3 copy.202
  490.5 1.3 copy.203
  491.8 115.0 %all-gather.12.cloned.1.call-done = bf16[8,4,48,4096]{3,2,0,1:T(8,128)(2,1)} async-done(((bf16[8,1,48,4096]{3,2,0,1:T(8,128)(2,1)}), bf16[8,4,48,4096]{3,2,0,1:T(8,128)(2,1)}) %all-gather.12.cloned.1.call-update) | async-done | bytes 12582928 | tf_op jit(solution)/shard_map/all_gather | solution.py:126
  606.8 17.4 %convert_bitcast_fusion = bf16[8,4,48,4096]{3,1,2,0:T(4,128)(2,1)} fusion(bf16[8,4,48,4096]{3,2,0,1:T(8,128)(2,1)} %all-gather.12.cloned.1.call-done, s32[4]{0:T(128)S(1)} %multiply_subtract_fusion.3, s32[]{:T(128)S(6)} %axis_index.15), kind=kOutput, calls=%fused_computation.4 | convolution fusion | flops 56623168 | bytes 25165844 | tf_op jit(solution)/shard_map/ij,sicp->sjcp/dot_general | solution.py:132
  624.2 23.3 %fusion.59 = f32[1,48,48]{2,1,0:T(8,128)S(1)} fusion(bf16[8,4,48,4096]{3,2,0,1:T(8,128)(2,1)} %all-gather.10.cloned.1.call-done, bf16[8,4,48,4096]{3,1,2,0:T(4,128)(2,1)} %convert_bitcast_fusion), kind=kOutput, calls=%fused_computation.95 | convolution fusion | flops 603979776 | bytes 25175040 | tf_op jit(solution)/shard_map/sjcp,sjop->co/dot_general | solution.py:164
  647.5 28.5 %psum.7 = f32[1,48,48]{2,1,0:T(8,128)S(1)} all-reduce(f32[1,48,48]{2,1,0:T(8,128)S(1)} %fusion.59), channel_id=1, replica_groups=mesh['blade'=4,'dp'=8] {'dp'}, use_global_device_ids=true, to_apply=%region_4.5 | all-reduce | flops 2304 | bytes 18432 | tf_op jit(solution)/shard_map/psum | solution.py:167
  676.7 12.8 %fusion.16 = f32[8,1,48,4096]{3,2,1,0:T(8,128)} fusion(f32[8,48,4096]{2,1,0:T(8,128)} %fusion.62, bf16[8,4,48,4096]{3,2,0,1:T(8,128)(2,1)} %all-gather.12.cloned.1.call-done, bf16[8,1,48,4096]{3,2,1,0:T(8,128)(2,1)} %param.11, f32[8]{0:T(128)S(1)} %select_reduce_fusion, bf16[4,48,48]{2,0,1:T(4,128)(2,1)S(1)} %convolution_convert_fusion.1), kind=kOutput, calls=%fused_computation.23 | convolution fusion | flops 610271232 | bytes 28330016 | tf_op jit(solution)/shard_map/siop,ico->scp/dot_general | solution.py:172
  (82 shorter events, 19.7 us)
Async XLA Ops:
  7.2 60.3 %all-gather.14.cloned.1.call-start = ((), (), s32[]{:S(2)}) async-start(), calls=%async_computation.6 | async-start | bytes 1966080 | tf_op jit(solution)/shard_map/all_gather | solution.py:92
  10.8 16.9 %copy-start.11 = (bf16[8,1,48,4096]{3,2,0,1:T(8,128)(2,1)}, bf16[8,1,48,4096]{3,2,0,1:T(8,128)(2,1)S(1)}, u32[]{:S(2)}) copy-start(bf16[8,1,48,4096]{3,2,0,1:T(8,128)(2,1)S(1)} %fusion.30) | copy-start | bytes 9437188
  27.7 2.0 copy-start.9
  27.7 3.2 copy-start.10
  33.6 100.8 %all-gather.8.cloned.1.call-start = ((), (), s32[]{:S(2)}) async-start(), calls=%async_computation.3 | async-start | bytes 7077888 | tf_op jit(solution)/shard_map/all_gather | solution.py:96
  36.1 161.7 %reduce-scatter.12.cloned.1.call-start = ((), (), s32[]{:S(2)}) async-start(), calls=%async_computation.9 | async-start | bytes 3932160
  73.7 63.6 %copy-start.1 = (bf16[8,4,48,256]{2,0,1,3:T(8,128)(2,1)}, bf16[8,4,48,256]{2,0,1,3:T(8,128)(2,1)S(1)}, u32[]{:S(2)}) copy-start(bf16[8,4,48,256]{2,0,1,3:T(8,128)(2,1)S(1)} %copy.222) | copy-start | bytes 2359300
  134.4 3.7 copy-start
  138.1 1.6 copy-start.3
  154.9 0.7 copy-start.15
  155.0 167.0 %all-gather.10.cloned.1.call-start = ((), (), s32[]{:S(2)}) async-start(), calls=%async_computation.4 | async-start | bytes 15728640 | tf_op jit(solution)/shard_map/all_gather | solution.py:90
  155.6 225.9 %all-gather.16.cloned.1.call-start = ((), (), s32[]{:S(2)}) async-start(), calls=%async_computation.7 | async-start | bytes 1966080 | tf_op jit(solution)/shard_map/all_gather | solution.py:127
  343.2 7.1 %copy-start.14 = (bf16[8,1,48,4096]{3,2,0,1:T(8,128)(2,1)}, bf16[8,1,48,4096]{3,2,0,1:T(8,128)(2,1)S(1)}, u32[]{:S(2)}) copy-start(bf16[8,1,48,4096]{3,2,0,1:T(8,128)(2,1)S(1)} %get-tuple-element.54) | copy-start | bytes 9437188
  350.3 98.5 %reduce-scatter.14.cloned.1.call-start = ((), (), s32[]{:S(2)}) async-start(), calls=%async_computation.10 | async-start | bytes 1966080
  385.9 13.8 %slice-start = ((s8[6291456]{0:T(1024)(128)(4,1)}), s8[2097152]{0:T(1024)(128)(4,1)S(1)}, s32[]{:S(2)}) async-start(s8[6291456]{0:T(1024)(128)(4,1)} %bitcast.210), calls=%async_computation.11 | async-start | bytes 4194304
  395.2 4.4 slice-start.1
  395.2 4.4 copy-start.7
  401.4 1.8 copy-start.5
  407.8 5.7 copy-start.2
  413.4 69.6 %reduce-scatter.10.cloned.1.call-start = ((), (), s32[]{:S(2)}) async-start(), calls=%async_computation.8 | async-start | bytes 2654208
  413.6 2.8 copy-start.8
  416.4 1.6 copy-start.4
  418.0 1.6 copy-start.6
  438.7 1.9 copy-start.12
  438.7 168.1 %all-gather.12.cloned.1.call-start = ((), (), s32[]{:S(2)}) async-start(), calls=%async_computation.5 | async-start | bytes 15728640 | tf_op jit(solution)/shard_map/all_gather | solution.py:126
  450.4 34.3 %copy-start.13 = (f32[1,32,2,48,48]{4,3,2,1,0:T(8,128)S(1)}, f32[1,32,2,48,48]{4,3,2,1,0:T(8,128)}, u32[]{:S(2)}) copy-start(f32[1,32,2,48,48]{4,3,2,1,0:T(8,128)} %param.14) | copy-start | bytes 1769476
  624.2 51.8 %copy-start.16 = (f32[1,48,48]{2,1,0:T(8,128)S(1)}, f32[1,48,48]{2,1,0:T(8,128)}, u32[]{:S(2)}) copy-start(f32[1,48,48]{2,1,0:T(8,128)} %param.18) | copy-start | bytes 27652
  624.2 51.8 %copy-start.17 = (f32[1,48,48]{2,1,0:T(8,128)S(1)}, f32[1,48,48]{2,1,0:T(8,128)}, u32[]{:S(2)}) copy-start(f32[1,48,48]{2,1,0:T(8,128)} %param.19) | copy-start | bytes 27652
Sparse Core Ops, SparseCore 0:
  33.7 33.6 all-gather.13
  69.6 64.7 all-gather.7
  155.1 42.6 reduce-scatter.11
  199.5 122.4 all-gather.9
  350.5 30.9 all-gather.15
  413.5 30.8 reduce-scatter.13
  446.7 36.1 reduce-scatter.9
  484.8 121.9 all-gather.11
where the time goes:
time: 706 us; the launch traced here: 697 us
  waiting for transfers between devices  406 us (58%)
  matrix products  128 us (18%)
  local copies, waits for them, and re-layouts  69 us (10%)
  other arithmetic  41 us (6%)
  blocking collectives  37.1 us (5%)
  between operations  15.1 us (2%)
    all_gather x1, waiting for transfers between devices, body(): lax.all_gather(grad_pre, 'blade', axis=1, tiled=True)  115 us
    all_gather x1, waiting for transfers between devices, body(): lax.all_gather(normed_low, 'blade', axis=1, tiled=True)  114 us
    unnamed x11, waiting for transfers between devices  58.4 us
    all_gather x1, waiting for transfers between devices, body(): block_in = lax.all_gather(spec_low, 'dp', axis=1, tiled=True)  56.9 us
    unnamed x49, local copies, waits for them, and re-layouts  38.6 us
    all_gather x1, waiting for transfers between devices, body(): lax.all_gather(own_modes, 'blade', axis=1, tiled=True)  31.1 us
    all_gather x1, waiting for transfers between devices, body(): lax.all_gather(grad_spec, 'blade', axis=1, tiled=True)  30.7 us
    psum x1, blocking collectives, body(): lin_grad = lax.psum(lin_grad, 'dp')  28.5 us
  transfers between devices with their start and end apart: 8, of which 7 were waited for; matrix products, arithmetic and copies ran while one was open for 11% of the time, Pallas kernels for 0%

commit v1 on v0

--- a/solution.py
+++ b/solution.py
@@ -16,6 +16,16 @@
 EPSILON = 1e-08
 RATE = 0.1
 DECAY = 0.01
+
+
+def gather_by_hops(array, axis, dim):
+    count = lax.axis_size(axis)
+    current, tiles = (array, [array])
+    for _ in range(count - 1):
+        current = lax.ppermute(current, axis, [(i, (i + 1) % count) for i in range(count)])
+        tiles.insert(0, current)
+    line = jnp.concatenate(tiles, axis=dim)
+    return jnp.roll(line, (lax.axis_index(axis) + 1) * array.shape[dim], axis=dim)
 
 
 def blade_sign(left_blade, right_blade):
@@ -93,7 +103,7 @@
     )
     modes_real = modes_all[..., :MODES]
     modes_imag = modes_all[..., MODES:]
-    block_in = lax.all_gather(spec_low, "dp", axis=1, tiled=True)
+    block_in = gather_by_hops(spec_low, "dp", 1)
     w_real = block_in[0, :, 0]
     w_imag = block_in[0, :, 1]
     form = partial(jnp.einsum, "sjcm,mco->sjom", preferred_element_type=jnp.float32)

time: 706 us -> 777 us (1.10)
  waiting for transfers between devices: 406 us -> 445 us
  local copies, waits for them, and re-layouts: 69 us -> 90.6 us
  matrix products: 128 us -> 140 us
    ppermute x0 -> x7, waiting for transfers between devices: none -> 73.4 us  [gather_by_hops(): lax.ppermute(current, axis, [(i, (i + 1) % count) for i in range(count)])]
    all_gather x1, waiting for transfers between devices: 31.1 us -> 0.71 us  [body(): lax.all_gather(own_modes, 'blade', axis=1, tiled=True)]
    unnamed x49 -> x76, local copies, waits for them, and re-layouts: 38.6 us -> 59.1 us
  transfers between devices with their start and end apart: 8 -> 15, of which waited for: 7 -> 13; matrix products, arithmetic and copies ran while one was open for 11% -> 17% of each run, Pallas kernels for 0% -> 0%
where the time goes in v1:
time: 777 us; the launch traced here: 770 us
  waiting for transfers between devices  445 us (57%)
  matrix products  140 us (18%)
  local copies, waits for them, and re-layouts  90.6 us (12%)
  other arithmetic  40.8 us (5%)
  blocking collectives  37.1 us (5%)
  between operations  15.1 us (2%)
    all_gather x1, waiting for transfers between devices, body(): lax.all_gather(grad_pre, 'blade', axis=1, tiled=True)  115 us
    all_gather x1, waiting for transfers between devices, body(): lax.all_gather(normed_low, 'blade', axis=1, tiled=True)  114 us
    ppermute x7, waiting for transfers between devices, gather_by_hops(): lax.ppermute(current, axis, [(i, (i + 1) % count) for i in range(count)])  73.4 us
    unnamed x11, waiting for transfers between devices  59.6 us
    unnamed x76, local copies, waits for them, and re-layouts  59.1 us
    all_gather x1, waiting for transfers between devices, body(): block_in = lax.all_gather(spec_low, 'dp', axis=1, tiled=True)  52.6 us
    all_gather x1, waiting for transfers between devices, body(): lax.all_gather(grad_spec, 'blade', axis=1, tiled=True)  30.1 us
    psum x1, blocking collectives, body(): lin_grad = lax.psum(lin_grad, 'dp')  28.5 us
  transfers between devices with their start and end apart: 15, of which 13 were waited for; matrix products, arithmetic and copies ran while one was open for 17% of the time, Pallas kernels for 0%

profile of v1, /device:TPU:0, one launch (start us, length us, event | category | flops | bytes accessed | tf_op | source)
XLA Modules:
  0.0 770.3 jit_solution(10138904560858856376)
XLA Ops:
  9.3 13.7 %collective-permute-done = bf16[1,32,2,48,48]{4,3,1,2,0:T(8,128)(2,1)S(1)} collective-permute-done((bf16[1,32,2,48,48]{4,3,1,2,0:T(8,128)(2,1)S(1)}, bf16[1,32,2,48,48]{4,3,1,2,0:T(8,128)(2,1)S(1)}, u32[]{:S(2)}, u32[]{:S(2)}) %collective-permute-start) | collective-permute-done | bytes 294944 | tf_op jit(solution)/shard_map/ppermute | solution.py:25
  23.9 13.2 %collective-permute-done.1 = bf16[1,32,2,48,48]{4,3,1,2,0:T(8,128)(2,1)S(1)} collective-permute-done((bf16[1,32,2,48,48]{4,3,1,2,0:T(8,128)(2,1)S(1)}, bf16[1,32,2,48,48]{4,3,1,2,0:T(8,128)(2,1)S(1)}, u32[]{:S(2)}, u32[]{:S(2)}) %collective-permute-start.1) | collective-permute-done | bytes 294944 | tf_op jit(solution)/shard_map/ppermute | solution.py:25
  38.0 13.2 %collective-permute-done.2 = bf16[1,32,2,48,48]{4,3,1,2,0:T(8,128)(2,1)S(1)} collective-permute-done((bf16[1,32,2,48,48]{4,3,1,2,0:T(8,128)(2,1)S(1)}, bf16[1,32,2,48,48]{4,3,1,2,0:T(8,128)(2,1)S(1)}, u32[]{:S(2)}, u32[]{:S(2)}) %collective-permute-start.2) | collective-permute-done | bytes 294944 | tf_op jit(solution)/shard_map/ppermute | solution.py:25
  52.1 13.2 %collective-permute-done.3 = bf16[1,32,2,48,48]{4,3,1,2,0:T(8,128)(2,1)S(1)} collective-permute-done((bf16[1,32,2,48,48]{4,3,1,2,0:T(8,128)(2,1)S(1)}, bf16[1,32,2,48,48]{4,3,1,2,0:T(8,128)(2,1)S(1)}, u32[]{:S(2)}, u32[]{:S(2)}) %collective-permute-start.3) | collective-permute-done | bytes 294944 | tf_op jit(solution)/shard_map/ppermute | solution.py:25
  65.3 19.3 %fusion.46 = (f32[4096,256]{1,0:T(8,128)}, f32[4096,256]{1,0:T(8,128)}) fusion(s32[256]{0:T(256)S(1)} %get-tuple-element.66, s32[4096]{0:T(1024)S(1)} %get-tuple-element.63, s32[256]{0:T(256)S(1)} %get-tuple-element.65, s32[4096]{0:T(1024)S(1)} %get-tuple-element.64), kind=kLoop, calls=%fused_computation.81 | loop fusion | flops 17825792 | bytes 8423424 | tf_op jit(solution)/shard_map/cos | solution.py:45
  85.7 12.7 %collective-permute-done.5 = bf16[1,32,2,48,48]{4,3,1,2,0:T(8,128)(2,1)} collective-permute-done((bf16[1,32,2,48,48]{4,3,1,2,0:T(8,128)(2,1)}, bf16[1,32,2,48,48]{4,3,1,2,0:T(8,128)(2,1)}, u32[]{:S(2)}, u32[]{:S(2)}) %collective-permute-start.5) | collective-permute-done | bytes 294944 | tf_op jit(solution)/shard_map/ppermute | solution.py:25
  98.4 6.0 fusion.57
  104.6 7.4 collective-permute-done.6
  111.9 2.2 constant_dynamic-update-slice_fusion.15
  114.2 2.2 constant_dynamic-update-slice_fusion.14
  118.5 2.2 constant_dynamic-update-slice_fusion.12
  137.3 2.4 fusion.124
  139.7 4.0 copy.259
  143.7 3.8 copy.258
  147.5 2.8 fusion.42
  150.3 3.0 fusion.45
  153.3 2.8 add_bitcast_fusion
  156.2 2.8 subtract_bitcast_fusion
  159.0 3.0 pad_maximum_fusion.1
  162.0 7.1 copy.203
  169.1 2.5 convolution_bitcast_fusion
  171.6 2.6 copy.205
  175.1 8.6 %all_gather.19 = bf16[4,48,48]{2,1,0:T(8,128)(2,1)S(1)} all-gather(bf16[1,48,48]{2,1,0:T(8,128)(2,1)S(1)} %convert_element_type.106), channel_id=1, replica_groups=mesh['blade'=4,'dp'=8] {'blade'}, dimensions={0}, use_global_device_ids=true | all-gather | bytes 23040 | tf_op jit(solution)/shard_map/all_gather | solution.py:101
  184.1 34.4 %reduce-scatter.12.cloned.1.call-done = f32[8,1,48,2,256]{4,2,3,0,1:T(8,128)} async-done(((f32[8,4,48,2,256]{4,2,3,0,1:T(8,128)}), f32[8,1,48,2,256]{4,2,3,0,1:T(8,128)}) %reduce-scatter.12.cloned.1.call-update) | async-done | bytes 786448
  220.3 8.8 %fusion.70 = f32[8,48,4096]{2,1,0:T(8,128)} fusion(bf16[8,48,512]{2,1,0:T(8,128)(2,1)S(1)} %convert_element_type.103, f32[4096,256]{1,0:T(8,128)} %get-tuple-element.61, f32[4096,256]{1,0:T(8,128)} %get-tuple-element.60, f32[512]{0:T(512)S(1)} %maximum_multiply_fusion), kind=kOutput, calls=%fused_computation.103 | convolution fusion | flops 1616904192 | bytes 15075328 | tf_op jit(solution)/shard_map/sjcn,pn->sjcp/dot_general | solution.py:117
  229.1 113.8 %all-gather.8.cloned.1.call-done = bf16[8,4,48,4096]{3,2,0,1:T(8,128)(2,1)} async-done(((bf16[8,1,48,4096]{3,2,0,1:T(8,128)(2,1)}), bf16[8,4,48,4096]{3,2,0,1:T(8,128)(2,1)}) %all-gather.8.cloned.1.call-update) | async-done | bytes 12582928 | tf_op jit(solution)/shard_map/all_gather | solution.py:100
  342.9 22.7 %fusion.12 = (bf16[8,1,48,4096]{3,2,0,1:T(8,128)(2,1)}, f32[8,48,4096]{2,1,0:T(8,128)}, f32[8,48,4096]{2,1,0:T(8,128)}) fusion(bf16[8,1,48,4096]{3,2,1,0:T(8,128)(2,1)} %param.11, f32[8,48,4096]{2,1,0:T(8,128)} %fusion.70, bf16[8,4,48,4096]{3,2,0,1:T(8,128)(2,1)} %all-gather.8.cloned.1.call-done, bf16[4,48,48]{1,2,0:T(8,128)(2,1)S(1)} %copy.209), kind=kOutput, calls=%fused_computation.19 | convolution fusion | flops 720371712 | bytes 37767168 | tf_op jit(solution)/shard_map/sjcp,jco->sop/dot_general | solution.py:124
  365.5 6.9 fusion.60
  373.5 30.1 %all-gather.16.cloned.1.call-done = bf16[8,192,512]{2,1,0:T(8,128)(2,1)} async-done(((bf16[8,48,512]{2,1,0:T(8,128)(2,1)}), bf16[8,192,512]{2,1,0:T(8,128)(2,1)}) %all-gather.16.cloned.1.call-update) | async-done | bytes 1572880 | tf_op jit(solution)/shard_map/all_gather | solution.py:137
  403.6 2.8 fusion.54
  408.0 5.2 copy.218
  413.2 4.0 copy.217
  417.2 52.6 %all-gather.12.cloned.1.call-done = bf16[1,256,2,48,48]{4,3,1,2,0:T(8,128)(2,1)} async-done(((bf16[1,32,2,48,48]{4,3,1,2,0:T(8,128)(2,1)}), bf16[1,256,2,48,48]{4,3,1,2,0:T(8,128)(2,1)}) %all-gather.12.cloned.1.call-update) | async-done | bytes 2359312 | tf_op jit(solution)/shard_map/all_gather | solution.py:158
  469.8 4.4 fusion.38
  480.0 2.9 pad_maximum_fusion.3
  482.9 5.3 copy.221
  488.5 3.4 fusion.126
  497.3 3.7 copy.256
  501.0 12.9 %reshape.321 = bf16[256,4608]{1,0:T(8,128)(2,1)} reshape(bf16[256,2,48,48]{3,2,1,0:T(8,128)(2,1)} %copy.256) | data formatting | bytes 4718592
  515.0 8.2 %fusion.37 = bf16[8,1,48,4096]{3,2,1,0:T(8,128)(2,1)} fusion(f32[8,48,4096]{2,1,0:T(8,128)} %get-tuple-element.55, f32[8,48,4096]{2,1,0:T(8,128)} %get-tuple-element.62, f32[8]{0:T(128)S(1)} %select_reduce_fusion, bf16[8,1,48,4096]{3,2,1,0:T(8,128)(2,1)S(1)} %copy-done.11), kind=kLoop, calls=%fused_computation.71 | loop fusion | flops 9437184 | bytes 18874400
  524.9 8.3 %fusion.66 = f32[8,48,4096]{2,1,0:T(8,128)} fusion(bf16[8,48,512]{2,1,0:T(8,128)(2,1)S(1)} %convert_element_type.117, f32[4096,256]{1,0:T(8,128)} %get-tuple-element.61, f32[4096,256]{1,0:T(8,128)} %get-tuple-element.60), kind=kOutput, calls=%fused_computation.102 | convolution fusion | flops 1616904192 | bytes 15073280 | tf_op jit(solution)/shard_map/sjcn,pn->sjcp/dot_general | solution.py:171
  533.2 23.4 %reduce-scatter.10.cloned.1.call-done = bf16[32,4608]{1,0:T(8,128)(2,1)} async-done(((bf16[256,4608]{1,0:T(8,128)(2,1)}), bf16[32,4608]{1,0:T(8,128)(2,1)}) %reduce-scatter.10.cloned.1.call-update) | async-done | bytes 294928
  558.3 3.1 multiply_subtract_fusion
  565.4 114.8 %all-gather.10.cloned.1.call-done = bf16[8,4,48,4096]{3,2,0,1:T(8,128)(2,1)} async-done(((bf16[8,1,48,4096]{3,2,0,1:T(8,128)(2,1)}), bf16[8,4,48,4096]{3,2,0,1:T(8,128)(2,1)}) %all-gather.10.cloned.1.call-update) | async-done | bytes 12582928 | tf_op jit(solution)/shard_map/all_gather | solution.py:136
  680.2 17.4 %convert_bitcast_fusion = bf16[8,4,48,4096]{3,1,2,0:T(4,128)(2,1)} fusion(bf16[8,4,48,4096]{3,2,0,1:T(8,128)(2,1)} %all-gather.10.cloned.1.call-done, s32[4]{0:T(128)S(1)} %multiply_subtract_fusion.3, s32[]{:T(128)S(6)} %axis_index.25), kind=kOutput, calls=%fused_computation.4 | convolution fusion | flops 56623168 | bytes 25165844 | tf_op jit(solution)/shard_map/ij,sicp->sjcp/dot_general | solution.py:142
  697.7 23.3 %fusion.63 = f32[1,48,48]{2,1,0:T(8,128)S(1)} fusion(bf16[8,4,48,4096]{3,2,0,1:T(8,128)(2,1)} %all-gather.8.cloned.1.call-done, bf16[8,4,48,4096]{3,1,2,0:T(4,128)(2,1)} %convert_bitcast_fusion), kind=kOutput, calls=%fused_computation.101 | convolution fusion | flops 603979776 | bytes 25175040 | tf_op jit(solution)/shard_map/sjcp,sjop->co/dot_general | solution.py:174
  720.9 28.5 %psum.7 = f32[1,48,48]{2,1,0:T(8,128)S(1)} all-reduce(f32[1,48,48]{2,1,0:T(8,128)S(1)} %fusion.63), channel_id=1, replica_groups=mesh['blade'=4,'dp'=8] {'dp'}, use_global_device_ids=true, to_apply=%region_4.5 | all-reduce | flops 2304 | bytes 18432 | tf_op jit(solution)/shard_map/psum | solution.py:177
  750.1 12.8 %fusion.16 = f32[8,1,48,4096]{3,2,1,0:T(8,128)} fusion(f32[8,48,4096]{2,1,0:T(8,128)} %fusion.66, bf16[8,4,48,4096]{3,2,0,1:T(8,128)(2,1)} %all-gather.10.cloned.1.call-done, bf16[8,1,48,4096]{3,2,1,0:T(8,128)(2,1)} %param.11, f32[8]{0:T(128)S(1)} %select_reduce_fusion, bf16[4,48,48]{2,0,1:T(4,128)(2,1)S(1)} %convolution_convert_fusion.1), kind=kOutput, calls=%fused_computation.23 | convolution fusion | flops 610271232 | bytes 28330016 | tf_op jit(solution)/shard_map/siop,ico->scp/dot_general | solution.py:182
  (123 shorter events, 50.6 us)
Async XLA Ops:
  7.2 77.4 %copy-start.24 = (f32[16]{0:T(128)S(1)}, f32[16]{0:T(128)}, u32[]{:S(2)}) copy-start(f32[16]{0:T(128)} %param.12) | copy-start | bytes 196
  7.2 77.4 %copy-start.25 = (s32[8]{0:T(128)S(1)}, s32[8]{0:T(128)}, u32[]{:S(2)}) copy-start(s32[8]{0:T(128)} %param.13) | copy-start | bytes 100
  7.2 130.1 %all-gather.14.cloned.1.call-start = ((), (), s32[]{:S(2)}) async-start(), calls=%async_computation.6 | async-start | bytes 1966080 | tf_op jit(solution)/shard_map/all_gather | solution.py:102
  8.7 76.1 %copy-start.20 = (bf16[1,32,2,48,48]{4,3,1,2,0:T(8,128)(2,1)}, bf16[1,32,2,48,48]{4,3,1,2,0:T(8,128)(2,1)S(1)}, u32[]{:S(2)}) copy-start(bf16[1,32,2,48,48]{4,3,1,2,0:T(8,128)(2,1)S(1)} %copy.290) | copy-start | bytes 884740
  8.8 76.1 %copy-start.10 = (bf16[8,1,48,4096]{3,2,1,0:T(8,128)(2,1)S(1)}, bf16[8,1,48,4096]{3,2,1,0:T(8,128)(2,1)}, u32[]{:S(2)}) copy-start(bf16[8,1,48,4096]{3,2,1,0:T(8,128)(2,1)} %param.10) | copy-start | bytes 9437188
  8.8 14.2 %collective-permute-start = (bf16[1,32,2,48,48]{4,3,1,2,0:T(8,128)(2,1)S(1)}, bf16[1,32,2,48,48]{4,3,1,2,0:T(8,128)(2,1)S(1)}, u32[]{:S(2)}, u32[]{:S(2)}) collective-permute-start(bf16[1,32,2,48,48]{4,3,1,2,0:T(8,128)(2,1)S(1)} %copy.290), channel_id=1, source_target_pairs={{0,1},{1,2},{2,3},{3,4},{4,5},{5,6},{6,7},{7,0},{8,9},{9,10},{10,1... | collective-permute-start | bytes 884744 | tf_op jit(solution)/shard_map/ppermute | solution.py:25
  23.0 0.9 copy-start.12
  23.9 13.2 %collective-permute-start.1 = (bf16[1,32,2,48,48]{4,3,1,2,0:T(8,128)(2,1)S(1)}, bf16[1,32,2,48,48]{4,3,1,2,0:T(8,128)(2,1)S(1)}, u32[]{:S(2)}, u32[]{:S(2)}) collective-permute-start(bf16[1,32,2,48,48]{4,3,1,2,0:T(8,128)(2,1)S(1)} %collective-permute-done), channel_id=1, source_target_pairs={{0,1},{1,2},{2,3},{3,4},{4,5},{5,6},{6,7},{7,0},{8,9},{9,10},{10,1... | collective-permute-start | bytes 884744 | tf_op jit(solution)/shard_map/ppermute | solution.py:25
  37.1 0.9 copy-start.14
  38.0 13.2 %collective-permute-start.2 = (bf16[1,32,2,48,48]{4,3,1,2,0:T(8,128)(2,1)S(1)}, bf16[1,32,2,48,48]{4,3,1,2,0:T(8,128)(2,1)S(1)}, u32[]{:S(2)}, u32[]{:S(2)}) collective-permute-start(bf16[1,32,2,48,48]{4,3,1,2,0:T(8,128)(2,1)S(1)} %collective-permute-done.1), channel_id=1, source_target_pairs={{0,1},{1,2},{2,3},{3,4},{4,5},{5,6},{6,7},{7,0},{8,9},{9,10},{10,1... | collective-permute-start | bytes 884744 | tf_op jit(solution)/shard_map/ppermute | solution.py:25
  51.2 0.9 copy-start.16
  52.1 13.2 %collective-permute-start.3 = (bf16[1,32,2,48,48]{4,3,1,2,0:T(8,128)(2,1)S(1)}, bf16[1,32,2,48,48]{4,3,1,2,0:T(8,128)(2,1)S(1)}, u32[]{:S(2)}, u32[]{:S(2)}) collective-permute-start(bf16[1,32,2,48,48]{4,3,1,2,0:T(8,128)(2,1)S(1)} %collective-permute-done.2), channel_id=1, source_target_pairs={{0,1},{1,2},{2,3},{3,4},{4,5},{5,6},{6,7},{7,0},{8,9},{9,10},{10,1... | collective-permute-start | bytes 884744 | tf_op jit(solution)/shard_map/ppermute | solution.py:25
  65.3 19.6 %copy-start.18 = (bf16[1,32,2,48,48]{4,3,1,2,0:T(8,128)(2,1)}, bf16[1,32,2,48,48]{4,3,1,2,0:T(8,128)(2,1)S(1)}, u32[]{:S(2)}) copy-start(bf16[1,32,2,48,48]{4,3,1,2,0:T(8,128)(2,1)S(1)} %collective-permute-done.3) | copy-start | bytes 884740
  65.3 19.5 %collective-permute-start.4 = (bf16[1,32,2,48,48]{4,3,1,2,0:T(8,128)(2,1)S(1)}, bf16[1,32,2,48,48]{4,3,1,2,0:T(8,128)(2,1)}, u32[]{:S(2)}, u32[]{:S(2)}) collective-permute-start(bf16[1,32,2,48,48]{4,3,1,2,0:T(8,128)(2,1)S(1)} %collective-permute-done.3), channel_id=1, source_target_pairs={{0,1},{1,2},{2,3},{3,4},{4,5},{5,6},{6,7},{7,0},{8,9},{9,10},{10,1... | collective-permute-start | bytes 884744 | tf_op jit(solution)/shard_map/ppermute | solution.py:25
  84.8 13.6 %collective-permute-start.5 = (bf16[1,32,2,48,48]{4,3,1,2,0:T(8,128)(2,1)}, bf16[1,32,2,48,48]{4,3,1,2,0:T(8,128)(2,1)}, u32[]{:S(2)}, u32[]{:S(2)}) collective-permute-start(bf16[1,32,2,48,48]{4,3,1,2,0:T(8,128)(2,1)} %collective-permute-done.4), channel_id=1, source_target_pairs={{0,1},{1,2},{2,3},{3,4},{4,5},{5,6},{6,7},{7,0},{8,9},{9,10},{10,1... | collective-permute-start | bytes 884744 | tf_op jit(solution)/shard_map/ppermute | solution.py:25
  85.7 12.7 %copy-start.9 = (bf16[8,1,48,4096]{3,2,0,1:T(8,128)(2,1)}, bf16[8,1,48,4096]{3,2,0,1:T(8,128)(2,1)S(1)}, u32[]{:S(2)}) copy-start(bf16[8,1,48,4096]{3,2,0,1:T(8,128)(2,1)S(1)} %fusion.30) | copy-start | bytes 9437188
  98.4 13.5 %collective-permute-start.6 = (bf16[1,32,2,48,48]{4,3,1,2,0:T(8,128)(2,1)}, bf16[1,32,2,48,48]{4,3,1,2,0:T(8,128)(2,1)}, u32[]{:S(2)}, u32[]{:S(2)}) collective-permute-start(bf16[1,32,2,48,48]{4,3,1,2,0:T(8,128)(2,1)} %collective-permute-done.5), channel_id=1, source_target_pairs={{0,1},{1,2},{2,3},{3,4},{4,5},{5,6},{6,7},{7,0},{8,9},{9,10},{10,1... | collective-permute-start | bytes 884744 | tf_op jit(solution)/shard_map/ppermute | solution.py:25
  104.4 17.4 %copy-start.15 = (bf16[1,32,2,48,48]{4,3,1,2,0:T(8,128)(2,1)S(1)}, bf16[1,32,2,48,48]{4,3,1,2,0:T(8,128)(2,1)}, u32[]{:S(2)}) copy-start(bf16[1,32,2,48,48]{4,3,1,2,0:T(8,128)(2,1)} %copy-done.14) | copy-start | bytes 884740
  104.4 18.4 %copy-start.13 = (bf16[1,32,2,48,48]{4,3,1,2,0:T(8,128)(2,1)S(1)}, bf16[1,32,2,48,48]{4,3,1,2,0:T(8,128)(2,1)}, u32[]{:S(2)}) copy-start(bf16[1,32,2,48,48]{4,3,1,2,0:T(8,128)(2,1)} %copy-done.12) | copy-start | bytes 884740
  104.4 19.5 %copy-start.6 = (f32[1,32,2,48,48]{4,3,2,1,0:T(8,128)S(1)}, f32[1,32,2,48,48]{4,3,2,1,0:T(8,128)}, u32[]{:S(2)}) copy-start(f32[1,32,2,48,48]{4,3,2,1,0:T(8,128)} %param.14) | copy-start | bytes 1769476
  104.5 114.0 %reduce-scatter.12.cloned.1.call-start = ((), (), s32[]{:S(2)}) async-start(), calls=%async_computation.9 | async-start | bytes 3932160
  104.5 16.2 %copy-start.17 = (bf16[1,32,2,48,48]{4,3,1,2,0:T(8,128)(2,1)S(1)}, bf16[1,32,2,48,48]{4,3,1,2,0:T(8,128)(2,1)}, u32[]{:S(2)}) copy-start(bf16[1,32,2,48,48]{4,3,1,2,0:T(8,128)(2,1)} %copy-done.16) | copy-start | bytes 884740
  120.7 10.7 %copy-start.19 = (bf16[1,32,2,48,48]{4,3,1,2,0:T(8,128)(2,1)S(1)}, bf16[1,32,2,48,48]{4,3,1,2,0:T(8,128)(2,1)}, u32[]{:S(2)}) copy-start(bf16[1,32,2,48,48]{4,3,1,2,0:T(8,128)(2,1)} %copy-done.18) | copy-start | bytes 884740
  150.3 3.0 copy-start
  171.6 3.5 copy-start.21
  174.3 168.6 %all-gather.8.cloned.1.call-start = ((), (), s32[]{:S(2)}) async-start(), calls=%async_computation.3 | async-start | bytes 15728640 | tf_op jit(solution)/shard_map/all_gather | solution.py:100
  175.0 228.6 %all-gather.16.cloned.1.call-start = ((), (), s32[]{:S(2)}) async-start(), calls=%async_computation.7 | async-start | bytes 1966080 | tf_op jit(solution)/shard_map/all_gather | solution.py:137
  372.4 97.3 %all-gather.12.cloned.1.call-start = ((), (), s32[]{:S(2)}) async-start(), calls=%async_computation.5 | async-start | bytes 7077888 | tf_op jit(solution)/shard_map/all_gather | solution.py:158
  373.0 150.2 %reduce-scatter.14.cloned.1.call-start = ((), (), s32[]{:S(2)}) async-start(), calls=%async_computation.10 | async-start | bytes 1966080
  469.8 4.4 copy-start.4
  469.8 5.0 copy-start.8
  476.5 1.8 copy-start.2
  488.2 68.4 %reduce-scatter.10.cloned.1.call-start = ((), (), s32[]{:S(2)}) async-start(), calls=%async_computation.8 | async-start | bytes 2654208
  488.5 3.4 copy-start.1
  488.5 3.5 copy-start.5
  493.0 1.7 copy-start.3
  501.0 14.0 %copy-start.11 = (bf16[8,1,48,4096]{3,2,1,0:T(8,128)(2,1)S(1)}, bf16[8,1,48,4096]{3,2,1,0:T(8,128)(2,1)}, u32[]{:S(2)}) copy-start(bf16[8,1,48,4096]{3,2,1,0:T(8,128)(2,1)} %param.10) | copy-start | bytes 9437188
  513.9 166.3 %all-gather.10.cloned.1.call-start = ((), (), s32[]{:S(2)}) async-start(), calls=%async_computation.4 | async-start | bytes 15728640 | tf_op jit(solution)/shard_map/all_gather | solution.py:136
  524.9 33.5 %copy-start.7 = (f32[1,32,2,48,48]{4,3,2,1,0:T(8,128)S(1)}, f32[1,32,2,48,48]{4,3,2,1,0:T(8,128)}, u32[]{:S(2)}) copy-start(f32[1,32,2,48,48]{4,3,2,1,0:T(8,128)} %param.14) | copy-start | bytes 1769476
  697.7 51.8 %copy-start.22 = (f32[1,48,48]{2,1,0:T(8,128)S(1)}, f32[1,48,48]{2,1,0:T(8,128)}, u32[]{:S(2)}) copy-start(f32[1,48,48]{2,1,0:T(8,128)} %param.18) | copy-start | bytes 27652
  697.7 51.8 %copy-start.23 = (f32[1,48,48]{2,1,0:T(8,128)S(1)}, f32[1,48,48]{2,1,0:T(8,128)}, u32[]{:S(2)}) copy-start(f32[1,48,48]{2,1,0:T(8,128)} %param.19) | copy-start | bytes 27652
Sparse Core Ops, SparseCore 0:
  104.6 32.6 all-gather.13
  174.4 44.0 reduce-scatter.11
  220.3 122.4 all-gather.7
  372.6 30.9 all-gather.15
  405.0 64.7 all-gather.11
  488.4 29.6 reduce-scatter.13
  520.3 36.2 reduce-scatter.9
  558.4 121.7 all-gather.9
